TPU v7x, 512 devices: a whole 4x4x16 slice. The times are simulated.
512 devices in a mesh: ctx: 32 (over x, y, core), head: 16 (over z).
Axes of the slice: x: 4, y: 4, z: 16, core: 2. Of those that a mesh axis runs over, the one named last changes fastest.
Arguments:
- mixed_in: bfloat16 [8192, 8192], P(('ctx', 'head')), may hold values from -6 to 6
- conv_weight: float32 [4, 8192], P(None, 'head'), may hold values from -3 to 3
- write_strength_logit: float32 [32, 8192], P('head', 'ctx'), may hold values from -10.5 to 2.2, as said below
- decay_log: float32 [32, 8192], P('head', 'ctx'), may hold values from -0.7 to 0, as said below
- initial_state: float32 [32, 128, 128], P('head'), may hold values from -6 to 6
- final_state_grad: float32 [32, 128, 128], P('head'), may hold values from -6 to 6
- grad_out: bfloat16 [8192, 4096], P('ctx', 'head'), may hold values from -6 to 6
Outputs:
- grad_mixed: bfloat16 [8192, 8192], P(('ctx', 'head'))
- grad_conv: float32 [4, 8192], P(None, 'head')
- grad_beta_logit: float32 [32, 8192], P('head', 'ctx')
- grad_decay_log: float32 [32, 8192], P('head', 'ctx')
Inputs may be any that keep to these rules, and one draw needn't show every extreme that they name: `write_strength_logit`: each value head's write strengths and decays vary from token to token. `decay_log`: every entry is negative.
All inputs are finite; a program needn't handle non-finite values.
Results may differ from a plain program's by a relative error of at most 0.001.
Values may be sent and summed in bfloat16 or wider, within the bound.
A program may use at most 64 MiB of HBM per device.

v0:
```python
import jax
import jax.numpy as jnp
from jax import lax
from jax.sharding import PartitionSpec as P

HK = 16
VALUE_HEADS = 32
DK = 128
DV = 128
KW = 4
BLOCK = 64
highest = lax.Precision.HIGHEST
norm_eps = 1e-06


def from_behind(value, axis, by):
    devices = lax.axis_size(axis)
    pairs = [(i, i + by) for i in range(devices) if 0 <= i + by < devices]
    return lax.ppermute(value, axis, pairs)


def prefix(value, axis, combine, identity, reverse):
    devices, mine = (lax.axis_size(axis), lax.axis_index(axis))
    everything = jax.tree.map(lambda part: lax.all_gather(part, axis), value)
    start = jax.tree.map(
        lambda part, zero: jnp.broadcast_to(jnp.asarray(zero, part.dtype), part.shape),
        value,
        identity,
    )

    def step(k, before):
        at = devices - 1 - k if reverse else k
        reached = at > mine if reverse else at < mine
        new = combine(before, jax.tree.map(lambda part: part[at], everything))
        return jax.tree.map(lambda a, b: jnp.where(reached, a, b), new, before)

    return lax.fori_loop(0, devices, step, start)


def block_step(carried, pieces):
    state, transit = carried
    queries, key_feats, values, beta_gate, log_decay = pieces
    block_size = log_decay.shape[0]
    cumulative = jnp.cumsum(log_decay)
    row_ids = lax.broadcasted_iota(jnp.int32, (block_size, block_size), 0)
    col_ids = lax.broadcasted_iota(jnp.int32, (block_size, block_size), 1)
    causal = col_ids <= row_ids
    differ = jnp.where(causal, cumulative[:, None] - cumulative[None, :], 0.0)
    ratios = jnp.where(causal, jnp.exp(differ), 0.0)
    key_gram = jnp.dot(key_feats, key_feats.T, precision=highest)
    lower_part = jnp.where(col_ids < row_ids, beta_gate[:, None] * ratios * key_gram, 0.0)
    system = lower_part + jnp.eye(block_size, dtype=jnp.float32)
    decays = jnp.exp(cumulative)
    right_sides = jnp.concatenate(
        [beta_gate[:, None] * values, (beta_gate * decays)[:, None] * key_feats], axis=1
    )
    solved = jax.scipy.linalg.solve_triangular(system, right_sides, lower=True)
    width_v = values.shape[1]
    base_update = solved[:, :width_v]
    weights = solved[:, width_v:]
    update = base_update - jnp.dot(weights, state, precision=highest)
    scores = ratios * jnp.dot(queries, key_feats.T, precision=highest)
    output = decays[:, None] * jnp.dot(queries, state, precision=highest) + jnp.dot(
        scores, update, precision=highest
    )
    total_decay = jnp.exp(cumulative[-1])
    tail_keys = jnp.exp(cumulative[-1] - cumulative)[:, None] * key_feats
    new_state = total_decay * state + jnp.dot(tail_keys.T, update, precision=highest)
    step_map = total_decay * jnp.eye(key_feats.shape[1], dtype=jnp.float32) - jnp.dot(
        tail_keys.T, weights, precision=highest
    )
    new_transit = jnp.dot(step_map, transit, precision=highest)
    return ((new_state, new_transit), output)


def run_head(state, queries, key_feats, values, beta_gate, log_decay):
    blocks = queries.shape[0] // BLOCK
    pieces = (
        queries.reshape(blocks, BLOCK, -1),
        key_feats.reshape(blocks, BLOCK, -1),
        values.reshape(blocks, BLOCK, -1),
        beta_gate.reshape(blocks, BLOCK),
        log_decay.reshape(blocks, BLOCK),
    )
    start = (state, jnp.eye(key_feats.shape[1], dtype=jnp.float32))
    (state_end, transit), outputs = lax.scan(block_step, start, pieces)
    return (outputs.reshape(-1, values.shape[1]), state_end, transit)


def normalize(feats, factor):
    return feats * lax.rsqrt(jnp.sum(feats * feats, axis=-1, keepdims=True) + norm_eps) * factor


def mix_layer(state_in, extended, conv_weight, write_strength_logit, decay_log):
    row_count = extended.shape[0] - (KW - 1)
    filtered_signal = conv_weight[0] * extended[0:row_count]
    for tap in range(1, KW):
        filtered_signal = filtered_signal + conv_weight[tap] * extended[tap : tap + row_count]
    activated = jax.nn.silu(filtered_signal)
    ratio_heads = VALUE_HEADS // HK
    group_width = 2 * DK + ratio_heads * DV
    groups = activated.reshape(row_count, -1, group_width)
    key_heads = groups.shape[1]
    queries = normalize(groups[:, :, :DK], DK ** (-0.5))
    key_feats = normalize(groups[:, :, DK : 2 * DK], 1.0)
    values = (
        groups[:, :, 2 * DK :].reshape(row_count, key_heads * ratio_heads, DV).transpose(1, 0, 2)
    )
    queries = jnp.repeat(queries.transpose(1, 0, 2), ratio_heads, axis=0)
    key_feats = jnp.repeat(key_feats.transpose(1, 0, 2), ratio_heads, axis=0)
    beta_gate = jax.nn.sigmoid(write_strength_logit)
    outputs, state_out, transit = jax.vmap(run_head)(
        state_in, queries, key_feats, values, beta_gate, decay_log
    )
    result = outputs.transpose(1, 0, 2).reshape(row_count, -1)
    return ((result, state_out), transit)


def compose(earlier, later):
    matrix = jnp.einsum("hij,hjk->hik", later[0], earlier[0], precision=highest)
    offset = jnp.einsum("hij,hjk->hik", later[0], earlier[1], precision=highest) + later[1]
    return (matrix, offset)


def advance(maps, state):
    return jnp.einsum("hij,hjk->hik", maps[0], state, precision=highest) + maps[1]


def on_device(
    mixed_in,
    conv_weight,
    write_strength_logit,
    decay_log,
    initial_state,
    final_state_grad,
    grad_out,
):
    local_in = lax.all_to_all(mixed_in, "head", split_axis=1, concat_axis=0, tiled=True)
    edge_rows = from_behind(local_in[-(KW - 1) :], "ctx", 1)
    extended = jnp.concatenate([edge_rows, local_in], axis=0).astype(jnp.float32)
    cotangent = grad_out.astype(jnp.float32)
    zeros_state = jnp.zeros_like(initial_state)

    def from_state(state):
        return mix_layer(state, extended, conv_weight, write_strength_logit, decay_log)

    primal, pull_state, transit = jax.vjp(from_state, zeros_state, has_aux=True)
    offset = primal[1]
    local_grad = pull_state((cotangent, jnp.zeros_like(offset)))[0]
    flipped = jnp.swapaxes(transit, 1, 2)
    identity = (
        jnp.broadcast_to(jnp.eye(transit.shape[1], dtype=jnp.float32), transit.shape),
        jnp.zeros_like(offset),
    )
    earlier_map = prefix((transit, offset), "ctx", compose, identity, False)
    later_map = prefix((flipped, local_grad), "ctx", compose, identity, True)
    state_in = advance(earlier_map, initial_state)
    state_grad = advance(later_map, final_state_grad)

    def forward(ext_rows, weight_taps, logits, decay_logs):
        return mix_layer(state_in, ext_rows, weight_taps, logits, decay_logs)

    unused, pull_all, unused_transit = jax.vjp(
        forward, extended, conv_weight, write_strength_logit, decay_log, has_aux=True
    )
    grad_ext, grad_weight, grad_beta, grad_decay = pull_all((cotangent, state_grad))
    spilled = from_behind(grad_ext[: KW - 1], "ctx", -1)
    own_grad = grad_ext[KW - 1 :]
    own_grad = jnp.concatenate([own_grad[: -(KW - 1)], own_grad[-(KW - 1) :] + spilled], axis=0)
    returned = lax.all_to_all(
        own_grad.astype(jnp.bfloat16), "head", split_axis=0, concat_axis=1, tiled=True
    )
    weight_total = lax.psum(grad_weight, "ctx")
    return (returned, weight_total, grad_beta, grad_decay)


def solution(mesh):
    in_specs = (
        P(("ctx", "head"), None),
        P(None, "head"),
        P("head", "ctx"),
        P("head", "ctx"),
        P("head", None, None),
        P("head", None, None),
        P("ctx", "head"),
    )
    out_specs = (P(("ctx", "head"), None), P(None, "head"), P("head", "ctx"), P("head", "ctx"))
    return jax.shard_map(
        on_device, mesh=mesh, in_specs=in_specs, out_specs=out_specs, check_vma=False
    )
```

profile of v0, /device:TPU:32, one launch (start us, length us, event | category | flops | bytes accessed | tf_op | source)
XLA Modules:
  0.0 795.1 jit_solution(5155768118002871086)
XLA Ops:
  7.2 1.7 copy.147
  8.9 15.2 %all-to-all-start = ((bf16[16,16,512]{2,0,1:T(8,128)(2,1)}), bf16[16,16,512]{2,0,1:T(8,128)(2,1)S(1)}, u32[]{:S(2)}, u32[]{:S(2)}) async-start(bf16[16,16,512]{2,0,1:T(8,128)(2,1)} %bitcast.435), calls=%async_computation | async-start | bytes 524288 | tf_op jit(solution)/shard_map/all_to_all | solution.py:138
  26.4 15.6 %all-to-all-done = bf16[16,16,512]{2,0,1:T(8,128)(2,1)S(1)} async-done(((bf16[16,16,512]{2,0,1:T(8,128)(2,1)}), bf16[16,16,512]{2,0,1:T(8,128)(2,1)S(1)}, u32[]{:S(2)}, u32[]{:S(2)}) %all-to-all-start) | async-done | bytes 262176 | tf_op jit(solution)/shard_map/all_to_all | solution.py:138
  48.5 65.6 %while.169 = (s32[]{:T(128)}, f32[2,128,128]{2,1,0:T(8,128)S(1)}, f32[2,128,128]{2,1,0:T(8,128)S(1)}, f32[4,2,64,128]{3,2,1,0:T(8,128)S(1)}, f32[4,2,64,1]{2,1,3...) while((s32[]{:T(128)}, f32[2,128,128]{2,1,0:T(8,128)S(1)}, ...), condition=%wide.region_4.6_spmd.clone.clone, body=%wide.region_2.5_spmd.clone.clone.sunk | while | flops 176640128 | bytes 2980628 | solution.py:86
  51.5 9.8 %custom-call.35 = f32[2,1,64,64]{2,3,1,0:T(8,128)S(1)} custom-call(f32[2,1,64,64]{3,2,1,0:T(8,128)S(1)} %fusion.420), custom_call_target="InvertDiagBlocksLowerTriangular" | custom-call | tf_op jit(solution)/shard_map/jvp(vmap())/while/body/eval_jaxpr/jit(_solve_triangular)/triangular_solve/custom-call.1 | solution.py:57
  67.9 9.8 %custom-call.35 = f32[2,1,64,64]{2,3,1,0:T(8,128)S(1)} custom-call(f32[2,1,64,64]{3,2,1,0:T(8,128)S(1)} %fusion.420), custom_call_target="InvertDiagBlocksLowerTriangular" | custom-call | tf_op jit(solution)/shard_map/jvp(vmap())/while/body/eval_jaxpr/jit(_solve_triangular)/triangular_solve/custom-call.1 | solution.py:57
  84.2 9.8 %custom-call.35 = f32[2,1,64,64]{2,3,1,0:T(8,128)S(1)} custom-call(f32[2,1,64,64]{3,2,1,0:T(8,128)S(1)} %fusion.420), custom_call_target="InvertDiagBlocksLowerTriangular" | custom-call | tf_op jit(solution)/shard_map/jvp(vmap())/while/body/eval_jaxpr/jit(_solve_triangular)/triangular_solve/custom-call.1 | solution.py:57
  100.7 9.8 %custom-call.35 = f32[2,1,64,64]{2,3,1,0:T(8,128)S(1)} custom-call(f32[2,1,64,64]{3,2,1,0:T(8,128)S(1)} %fusion.420), custom_call_target="InvertDiagBlocksLowerTriangular" | custom-call | tf_op jit(solution)/shard_map/jvp(vmap())/while/body/eval_jaxpr/jit(_solve_triangular)/triangular_solve/custom-call.1 | solution.py:57
  116.9 9.2 %while.166 = (s32[]{:T(128)}, f32[2,128,128]{2,1,0:T(8,128)S(1)}, f32[4,2,1,1]{1,3,2,0:T(1,128)S(1)}, f32[4,2,64,128]{3,2,1,0:T(8,128)S(1)}, f32[4,2,64,1]{2,1,3...) while((s32[]{:T(128)}, f32[2,128,128]{2,1,0:T(8,128)S(1)}, ...), condition=%wide.region_6.8_spmd.clone, body=%wide.region_5.7_spmd.clone.sunk | while | flops 88293376 | bytes 1316019 | solution.py:86
  128.2 45.1 %all-gather.9.cloned.1.call-done = f32[64,128,128]{2,1,0:T(8,128)} async-done(((f32[2,128,128]{2,1,0:T(8,128)}), f32[64,128,128]{2,1,0:T(8,128)}) %all-gather.9.cloned.1.call-update) | async-done | bytes 4194320 | tf_op jit(solution)/shard_map/all_gather | solution.py:24
  173.2 64.6 %all-gather.11.cloned.1.call-done = f32[64,128,128]{2,1,0:T(8,128)} async-done(((f32[2,128,128]{2,1,0:T(8,128)}), f32[64,128,128]{2,1,0:T(8,128)}) %all-gather.11.cloned.1.call-update) | async-done | bytes 4194320 | tf_op jit(solution)/shard_map/all_gather | solution.py:24
  237.9 80.1 %while.167 = (s32[]{:T(128)}, f32[2,128,128]{2,1,0:T(8,128)S(1)}, f32[2,128,128]{2,1,0:T(8,128)S(1)}, s32[]{:T(128)}, f32[32,2,128,128]{3,2,1,0:T(8,128)}, /*ind...) while((s32[]{:T(128)}, f32[2,128,128]{2,1,0:T(8,128)S(1)}, ...), condition=%wide.region_8.10_spmd.clone, body=%wide.region_7.9_spmd.clone.sunk | while | flops 100827144 | bytes 1706674 | solution.py:37
  318.0 47.8 %all-gather.15.cloned.1.call-done = f32[64,128,128]{2,1,0:T(8,128)} async-done(((f32[2,128,128]{2,1,0:T(8,128)}), f32[64,128,128]{2,1,0:T(8,128)}) %all-gather.15.cloned.1.call-update) | async-done | bytes 4194320 | tf_op jit(solution)/shard_map/all_gather | solution.py:24
  365.9 79.6 %while.168 = (s32[]{:T(128)}, f32[2,128,128]{2,1,0:T(8,128)S(1)}, f32[2,128,128]{2,1,0:T(8,128)S(1)}, s32[]{:T(128)}, f32[32,2,128,128]{3,2,1,0:T(8,128)}, /*ind...) while((s32[]{:T(128)}, f32[2,128,128]{2,1,0:T(8,128)S(1)}, f32[2,128,128]{2,1,0:T(8,128)S(1)}, ...), condition=%wide.region_10.12_spmd.clone, body=%wide.region_9.11_spmd.clone.sunk | while | flops 100827136 | bytes 1706612 | solution.py:37
  458.0 107.3 %while.164 = (s32[]{:T(128)}, f32[2,128,128]{2,1,0:T(8,128)S(1)}, f32[4,2,64,64]{3,2,1,0:T(8,128)}, f32[4,2,128,64]{2,3,1,0:T(8,128)}, f32[4,2,64,64]{3,2,1,0:T(...) while((s32[]{:T(128)}, f32[2,128,128]{2,1,0:T(8,128)S(1)}, ...), condition=%wide.region_13.15_spmd.clone.clone, body=%wide.region_11.14_spmd.clone.clone.sunk | while | flops 126194176 | bytes 3312057 | solution.py:86
  461.6 1.4 select_bitcast_fusion.4
  463.0 11.2 %custom-call.33 = f32[2,1,64,64]{2,3,1,0:T(8,128)} custom-call(f32[2,1,64,64]{3,2,1,0:T(8,128)} %select_bitcast_fusion.4), custom_call_target="InvertDiagBlocksLowerTriangular" | custom-call | tf_op jit(solution)/shard_map/jvp(vmap())/while/body/eval_jaxpr/jit(_solve_triangular)/triangular_solve/custom-call.1 | solution.py:57
  474.2 1.8 bitcast_dynamic-update-slice_fusion.22
  477.4 1.7 bitcast_dynamic-update-slice_fusion.24
  488.4 1.4 select_bitcast_fusion.4
  489.8 11.2 %custom-call.33 = f32[2,1,64,64]{2,3,1,0:T(8,128)} custom-call(f32[2,1,64,64]{3,2,1,0:T(8,128)} %select_bitcast_fusion.4), custom_call_target="InvertDiagBlocksLowerTriangular" | custom-call | tf_op jit(solution)/shard_map/jvp(vmap())/while/body/eval_jaxpr/jit(_solve_triangular)/triangular_solve/custom-call.1 | solution.py:57
  501.0 1.8 bitcast_dynamic-update-slice_fusion.22
  504.2 1.7 bitcast_dynamic-update-slice_fusion.24
  515.2 1.4 select_bitcast_fusion.4
  516.6 11.2 %custom-call.33 = f32[2,1,64,64]{2,3,1,0:T(8,128)} custom-call(f32[2,1,64,64]{3,2,1,0:T(8,128)} %select_bitcast_fusion.4), custom_call_target="InvertDiagBlocksLowerTriangular" | custom-call | tf_op jit(solution)/shard_map/jvp(vmap())/while/body/eval_jaxpr/jit(_solve_triangular)/triangular_solve/custom-call.1 | solution.py:57
  527.8 1.8 bitcast_dynamic-update-slice_fusion.22
  531.0 1.7 bitcast_dynamic-update-slice_fusion.24
  542.1 1.4 select_bitcast_fusion.4
  543.5 11.2 %custom-call.33 = f32[2,1,64,64]{2,3,1,0:T(8,128)} custom-call(f32[2,1,64,64]{3,2,1,0:T(8,128)} %select_bitcast_fusion.4), custom_call_target="InvertDiagBlocksLowerTriangular" | custom-call | tf_op jit(solution)/shard_map/jvp(vmap())/while/body/eval_jaxpr/jit(_solve_triangular)/triangular_solve/custom-call.1 | solution.py:57
  554.7 1.8 bitcast_dynamic-update-slice_fusion.22
  557.9 1.7 bitcast_dynamic-update-slice_fusion.24
  569.3 127.3 %while.165 = (s32[]{:T(128)}, f32[2,128,128]{2,1,0:T(8,128)S(1)}, f32[4,2,64,128]{3,2,1,0:T(8,128)}, f32[4,2,64,128]{3,2,1,0:T(8,128)}, f32[4,2,64,128]{3,2,0,1:...) while((s32[]{:T(128)}, f32[2,128,128]{2,1,0:T(8,128)S(1)}, ...), condition=%wide.region_25.27_spmd.clone.clone, body=%wide.region_14.26_spmd.clone.clone.sunk | while | flops 283857920 | bytes 5617773 | solution.py:86
  572.9 9.8 %custom-call.34 = f32[2,1,64,64]{2,3,1,0:T(8,128)S(1)} custom-call(f32[2,1,64,64]{3,2,1,0:T(8,128)S(1)} %select_bitcast_fusion.5), custom_call_target="InvertDiagBlocksLowerTriangular" | custom-call | tf_op jit(solution)/shard_map/transpose(jvp(vmap()))/while/body/eval_jaxpr/jit(_solve_triangular)/triangular_solve | solution.py:57
  591.1 1.7 fusion.375
  594.8 1.8 fusion.380
  604.8 9.8 %custom-call.34 = f32[2,1,64,64]{2,3,1,0:T(8,128)S(1)} custom-call(f32[2,1,64,64]{3,2,1,0:T(8,128)S(1)} %select_bitcast_fusion.5), custom_call_target="InvertDiagBlocksLowerTriangular" | custom-call | tf_op jit(solution)/shard_map/transpose(jvp(vmap()))/while/body/eval_jaxpr/jit(_solve_triangular)/triangular_solve | solution.py:57
  622.9 1.7 fusion.375
  626.6 1.8 fusion.380
  636.6 9.8 %custom-call.34 = f32[2,1,64,64]{2,3,1,0:T(8,128)S(1)} custom-call(f32[2,1,64,64]{3,2,1,0:T(8,128)S(1)} %select_bitcast_fusion.5), custom_call_target="InvertDiagBlocksLowerTriangular" | custom-call | tf_op jit(solution)/shard_map/transpose(jvp(vmap()))/while/body/eval_jaxpr/jit(_solve_triangular)/triangular_solve | solution.py:57
  654.8 1.7 fusion.375
  658.5 1.8 fusion.380
  668.4 9.8 %custom-call.34 = f32[2,1,64,64]{2,3,1,0:T(8,128)S(1)} custom-call(f32[2,1,64,64]{3,2,1,0:T(8,128)S(1)} %select_bitcast_fusion.5), custom_call_target="InvertDiagBlocksLowerTriangular" | custom-call | tf_op jit(solution)/shard_map/transpose(jvp(vmap()))/while/body/eval_jaxpr/jit(_solve_triangular)/triangular_solve | solution.py:57
  686.6 1.7 fusion.375
  690.3 1.8 fusion.380
  701.7 1.5 multiply_reduce_fusion.3
  705.2 1.4 collective-permute-done.1
  707.4 12.7 %all-to-all-start.1 = ((bf16[16,16,512]{2,1,0:T(8,128)(2,1)}), bf16[16,16,512]{2,1,0:T(8,128)(2,1)S(1)}, u32[]{:S(2)}, u32[]{:S(2)}) async-start(bf16[16,16,512]{2,1,0:T(8,128)(2,1)} %bitcast.32), calls=%async_computation.1 | async-start | bytes 524288 | tf_op jit(solution)/shard_map/all_to_all | solution.py:170
  720.8 66.5 %psum.7 = f32[4,512]{1,0:T(4,128)} all-reduce(f32[4,512]{1,0:T(4,128)S(1)} %pad_add_fusion.5), channel_id=1, replica_groups=mesh['ctx'=32,'head'=16] {'ctx'}, use_global_device_ids=true, to_apply=%region_34.36 | all-reduce | flops 2048 | bytes 16384 | tf_op jit(solution)/shard_map/psum | solution.py:173
  (724 shorter events, 346.5 us)
Async XLA Ops:
  7.2 438.4 %copy-start = (f32[2,128,128]{2,1,0:T(8,128)S(1)}, f32[2,128,128]{2,1,0:T(8,128)}, u32[]{:S(2)}) copy-start(f32[2,128,128]{2,1,0:T(8,128)} %param.25) | copy-start | bytes 393220
  8.9 33.1 %all-to-all-start = ((bf16[16,16,512]{2,0,1:T(8,128)(2,1)}), bf16[16,16,512]{2,0,1:T(8,128)(2,1)S(1)}, u32[]{:S(2)}, u32[]{:S(2)}) async-start(bf16[16,16,512]{2,0,1:T(8,128)(2,1)} %bitcast.435), calls=%async_computation | async-start | bytes 524288 | tf_op jit(solution)/shard_map/all_to_all | solution.py:138
  24.1 149.1 %all-gather.9.cloned.1.call-start = ((), (), s32[]{:S(2)}) async-start(), calls=%async_computation.2 | async-start | bytes 4325376 | tf_op jit(solution)/shard_map/all_gather | solution.py:24
  26.3 21.4 %copy-start.8 = (f32[1,512]{1,0:T(1,128)}, f32[1,512]{1,0:T(1,128)S(1)}, u32[]{:S(2)}) copy-start(f32[1,512]{1,0:T(1,128)S(1)} %get-tuple-element.3118) | copy-start | bytes 6148
  26.3 21.4 %copy-start.10 = (f32[1,512]{1,0:T(1,128)}, f32[1,512]{1,0:T(1,128)S(1)}, u32[]{:S(2)}) copy-start(f32[1,512]{1,0:T(1,128)S(1)} %get-tuple-element.3119) | copy-start | bytes 6148
  26.3 21.4 %copy-start.12 = (f32[1,512]{1,0:T(1,128)}, f32[1,512]{1,0:T(1,128)S(1)}, u32[]{:S(2)}) copy-start(f32[1,512]{1,0:T(1,128)S(1)} %get-tuple-element.3120) | copy-start | bytes 6148
  26.4 21.4 %copy-start.14 = (f32[1,512]{1,0:T(1,128)}, f32[1,512]{1,0:T(1,128)S(1)}, u32[]{:S(2)}) copy-start(f32[1,512]{1,0:T(1,128)S(1)} %get-tuple-element.3121) | copy-start | bytes 6148
  42.0 3.4 collective-permute-start
  46.7 0.6 copy-start.18
  46.7 1.8 copy-start.19
  47.3 1.3 copy-start.17
  48.5 66.4 %copy-start.5 = (bf16[256,256]{1,0:T(8,128)(2,1)S(1)}, bf16[256,256]{1,0:T(8,128)(2,1)}, u32[]{:S(2)}) copy-start(bf16[256,256]{1,0:T(8,128)(2,1)} %param.27) | copy-start | bytes 393220
  114.1 2.8 copy-start.2
  114.1 2.8 copy-start.3
  114.9 123.0 %all-gather.11.cloned.1.call-start = ((), (), s32[]{:S(2)}) async-start(), calls=%async_computation.3 | async-start | bytes 4325376 | tf_op jit(solution)/shard_map/all_gather | solution.py:24
  126.2 0.7 copy-start.1
  126.8 191.2 %all-gather.13.cloned.1.call-start = ((), (), s32[]{:S(2)}) async-start(), calls=%async_computation.4 | async-start | bytes 4325376 | tf_op jit(solution)/shard_map/all_gather | solution.py:24
  127.6 238.3 %all-gather.15.cloned.1.call-start = ((), (), s32[]{:S(2)}) async-start(), calls=%async_computation.5 | async-start | bytes 4325376 | tf_op jit(solution)/shard_map/all_gather | solution.py:24
  318.0 47.9 %copy-start.4 = (f32[2,128,128]{2,1,0:T(8,128)}, f32[2,128,128]{2,1,0:T(8,128)S(1)}, u32[]{:S(2)}) copy-start(f32[2,128,128]{2,1,0:T(8,128)S(1)} %get-tuple-element.2004) | copy-start | bytes 393220
  569.3 29.8 %copy-start.7 = (f32[4,2,64]{2,1,0:T(2,128)S(1)}, f32[4,2,64]{2,1,0:T(2,128)}, u32[]{:S(2)}) copy-start(f32[4,2,64]{2,1,0:T(2,128)} %get-tuple-element.4201) | copy-start | bytes 6148 | tf_op jit(solution)/shard_map/transpose(jvp(vmap()))/while
  569.3 30.1 %copy-start.6 = (f32[4,2,64]{2,1,0:T(2,128)S(1)}, f32[4,2,64]{2,1,0:T(2,128)}, u32[]{:S(2)}) copy-start(f32[4,2,64]{2,1,0:T(2,128)} %get-tuple-element.4198) | copy-start | bytes 6148 | tf_op jit(solution)/shard_map/transpose(jvp(vmap()))/while
  601.2 29.8 %copy-start.7 = (f32[4,2,64]{2,1,0:T(2,128)S(1)}, f32[4,2,64]{2,1,0:T(2,128)}, u32[]{:S(2)}) copy-start(f32[4,2,64]{2,1,0:T(2,128)} %get-tuple-element.4201) | copy-start | bytes 6148 | tf_op jit(solution)/shard_map/transpose(jvp(vmap()))/while
  601.2 30.0 %copy-start.6 = (f32[4,2,64]{2,1,0:T(2,128)S(1)}, f32[4,2,64]{2,1,0:T(2,128)}, u32[]{:S(2)}) copy-start(f32[4,2,64]{2,1,0:T(2,128)} %get-tuple-element.4198) | copy-start | bytes 6148 | tf_op jit(solution)/shard_map/transpose(jvp(vmap()))/while
  633.0 29.8 %copy-start.7 = (f32[4,2,64]{2,1,0:T(2,128)S(1)}, f32[4,2,64]{2,1,0:T(2,128)}, u32[]{:S(2)}) copy-start(f32[4,2,64]{2,1,0:T(2,128)} %get-tuple-element.4201) | copy-start | bytes 6148 | tf_op jit(solution)/shard_map/transpose(jvp(vmap()))/while
  633.0 30.0 %copy-start.6 = (f32[4,2,64]{2,1,0:T(2,128)S(1)}, f32[4,2,64]{2,1,0:T(2,128)}, u32[]{:S(2)}) copy-start(f32[4,2,64]{2,1,0:T(2,128)} %get-tuple-element.4198) | copy-start | bytes 6148 | tf_op jit(solution)/shard_map/transpose(jvp(vmap()))/while
  664.8 29.8 %copy-start.7 = (f32[4,2,64]{2,1,0:T(2,128)S(1)}, f32[4,2,64]{2,1,0:T(2,128)}, u32[]{:S(2)}) copy-start(f32[4,2,64]{2,1,0:T(2,128)} %get-tuple-element.4201) | copy-start | bytes 6148 | tf_op jit(solution)/shard_map/transpose(jvp(vmap()))/while
  664.8 30.1 %copy-start.6 = (f32[4,2,64]{2,1,0:T(2,128)S(1)}, f32[4,2,64]{2,1,0:T(2,128)}, u32[]{:S(2)}) copy-start(f32[4,2,64]{2,1,0:T(2,128)} %get-tuple-element.4198) | copy-start | bytes 6148 | tf_op jit(solution)/shard_map/transpose(jvp(vmap()))/while
  696.7 6.5 copy-start.9
  696.7 6.6 copy-start.11
  696.7 6.6 copy-start.13
  696.7 6.6 copy-start.15
  703.5 16.6 %copy-start.16 = (f32[4,2,64]{2,1,0:T(2,128)S(1)}, f32[4,2,64]{2,1,0:T(2,128)}, u32[]{:S(2)}) copy-start(f32[4,2,64]{2,1,0:T(2,128)} %get-tuple-element.2034) | copy-start | bytes 6148
  703.5 83.7 %copy-start.20 = (f32[2,256]{1,0:T(2,128)S(1)}, f32[2,256]{1,0:T(2,128)}, u32[]{:S(2)}) copy-start(f32[2,256]{1,0:T(2,128)} %param.23) | copy-start | bytes 6148
  703.6 3.1 collective-permute-start.1
  707.4 80.5 %all-to-all-start.1 = ((bf16[16,16,512]{2,1,0:T(8,128)(2,1)}), bf16[16,16,512]{2,1,0:T(8,128)(2,1)S(1)}, u32[]{:S(2)}, u32[]{:S(2)}) async-start(bf16[16,16,512]{2,1,0:T(8,128)(2,1)} %bitcast.32), calls=%async_computation.1 | async-start | bytes 524288 | tf_op jit(solution)/shard_map/all_to_all | solution.py:170
Sparse Core Ops, SparseCore 0:
  115.0 58.1 all-gather.8
  176.9 60.8 all-gather.10
  241.0 60.9 all-gather.12
  304.9 60.8 all-gather.14
where the time goes:
time: 802 us; the launch traced here: 795 us
  matrix products  258 us (32%)
  other arithmetic  180 us (22%)
  waiting for transfers between devices  176 us (22%)
  blocking collectives  66.5 us (8%)
  local copies, waits for them, and re-layouts  64.8 us (8%)
  starting transfers between devices  30.8 us (4%)
  between operations  14.3 us (2%)
    all_gather x4, waiting for transfers between devices, prefix(): everything = jax.tree.map(lambda part: lax.all_gather(part, axis), value)  158 us
    another operation x32, other arithmetic, block_step(): solved = jax.scipy.linalg.solve_triangular(system, right_sides, lower=True)  133 us
    dot_general x64, matrix products, compose(): jnp.einsum('hij,hjk->hik', later[0], earlier[1], precision=highest)  79.3 us
    dot_general x64, matrix products, compose(): matrix = jnp.einsum('hij,hjk->hik', later[0], earlier[0], precision=highest)  75.2 us
    psum x1, blocking collectives, on_device(): weight_total = lax.psum(grad_weight, 'ctx')  66.5 us
    dynamic_update_slice x24, other arithmetic, run_head(): (state_end, transit), outputs = lax.scan(block_step, start, pieces)  18.8 us
    dot_general x16, matrix products, block_step(): scores = ratios * jnp.dot(queries, key_feats.T, precision=highest)  18.5 us
    dot_general x20, matrix products, block_step(): jnp.dot(tail_keys.T, update, precision=highest)  17.8 us
  transfers between devices with their start and end apart: 8, of which 5 were waited for; matrix products, arithmetic and copies ran while one was open for 12% of the time, Pallas kernels for 0%

commit v1 on v0

--- a/solution.py
+++ b/solution.py
@@ -11,6 +11,22 @@
 BLOCK = 64
 highest = lax.Precision.HIGHEST
 norm_eps = 1e-06
+
+
+def exchange_in_pairs(shard, axis, split, join):
+    ways, here = (lax.axis_size(axis), lax.axis_index(axis))
+    width = shard.shape[split] // ways
+    shape = list(shard.shape)
+    shape[split] = width
+    height = shape[join]
+    shape[join] = height * ways
+    full = jnp.zeros(shape, shard.dtype)
+    for mask in range(ways):
+        part = lax.dynamic_slice_in_dim(shard, (here ^ mask) * width, width, axis=split)
+        if mask:
+            part = lax.ppermute(part, axis, [(d, d ^ mask) for d in range(ways)])
+        full = lax.dynamic_update_slice_in_dim(full, part, (here ^ mask) * height, axis=join)
+    return full
 
 
 def from_behind(value, axis, by):
@@ -135,7 +151,7 @@
     final_state_grad,
     grad_out,
 ):
-    local_in = lax.all_to_all(mixed_in, "head", split_axis=1, concat_axis=0, tiled=True)
+    local_in = exchange_in_pairs(mixed_in, "head", 1, 0)
     edge_rows = from_behind(local_in[-(KW - 1) :], "ctx", 1)
     extended = jnp.concatenate([edge_rows, local_in], axis=0).astype(jnp.float32)
     cotangent = grad_out.astype(jnp.float32)

time: 802 us -> 858 us (1.070)
  starting transfers between devices: 30.8 us -> 96.9 us
    ppermute x0 -> x15, starting transfers between devices: none -> 81.3 us  [exchange_in_pairs(): part = lax.ppermute(part, axis, [(d, d ^ mask) for d in range(ways)])]
    all_to_all x1 -> x0, waiting for transfers between devices: 15.6 us -> none  [on_device(): lax.all_to_all(mixed_in, 'head', split_axis=1, concat_axis=0, tiled=True)]
    all_to_all x1 -> x0, starting transfers between devices: 15.2 us -> none  [on_device(): lax.all_to_all(mixed_in, 'head', split_axis=1, concat_axis=0, tiled=True)]
  transfers between devices with their start and end apart: 8 -> 22, of which waited for: 5 -> 5; matrix products, arithmetic and copies ran while one was open for 12% -> 11% of each run, Pallas kernels for 0% -> 0%
where the time goes in v1:
time: 858 us; the launch traced here: 851 us
  matrix products  255 us (30%)
  other arithmetic  178 us (21%)
  waiting for transfers between devices  170 us (20%)
  starting transfers between devices  96.9 us (11%)
  blocking collectives  66.4 us (8%)
  local copies, waits for them, and re-layouts  65 us (8%)
  between operations  14.8 us (2%)
    all_gather x4, waiting for transfers between devices, prefix(): everything = jax.tree.map(lambda part: lax.all_gather(part, axis), value)  162 us
    another operation x32, other arithmetic, block_step(): solved = jax.scipy.linalg.solve_triangular(system, right_sides, lower=True)  133 us
    ppermute x15, starting transfers between devices, exchange_in_pairs(): part = lax.ppermute(part, axis, [(d, d ^ mask) for d in range(ways)])  81.3 us
    dot_general x64, matrix products, compose(): jnp.einsum('hij,hjk->hik', later[0], earlier[1], precision=highest)  79.3 us
    dot_general x64, matrix products, compose(): matrix = jnp.einsum('hij,hjk->hik', later[0], earlier[0], precision=highest)  75.3 us
    psum x1, blocking collectives, on_device(): weight_total = lax.psum(grad_weight, 'ctx')  66.4 us
    dot_general x16, matrix products, block_step(): scores = ratios * jnp.dot(queries, key_feats.T, precision=highest)  18.5 us
  transfers between devices with their start and end apart: 22, of which 5 were waited for; matrix products, arithmetic and copies ran while one was open for 11% of the time, Pallas kernels for 0%

profile of v1, /device:TPU:32, one launch (start us, length us, event | category | flops | bytes accessed | tf_op | source)
XLA Modules:
  0.0 850.9 jit_solution(382479350491450475)
XLA Ops:
  8.3 7.4 collective-permute-start
  15.7 1.9 collective-permute-start.1
  17.7 3.4 collective-permute-start.2
  21.1 6.0 collective-permute-start.3
  27.0 5.2 collective-permute-start.4
  34.5 6.4 collective-permute-start.5
  40.9 3.7 collective-permute-start.6
  44.6 11.4 %collective-permute-start.7 = (bf16[16,512]{1,0:T(8,128)(2,1)S(1)}, bf16[16,512]{1,0:T(8,128)(2,1)S(1)}, u32[]{:S(2)}, u32[]{:S(2)}) collective-permute-start(bf16[16,512]{1,0:T(8,128)(2,1)S(1)} %get-tuple-element.3222), channel_id=1, source_target_pairs={{0,8},{1,9},{2,10},{3,11},{4,12},{5,13},{6,14},{7,15},{8,0},{9,1},... | collective-permute-start | bytes 49160 | tf_op jit(solution)/shard_map/ppermute | solution.py:27
  56.0 4.7 collective-permute-start.8
  60.7 5.0 collective-permute-start.9
  65.7 6.4 collective-permute-start.10
  72.2 5.0 collective-permute-start.11
  77.2 6.1 collective-permute-start.12
  83.4 5.6 collective-permute-start.13
  89.0 3.3 collective-permute-start.14
  92.4 5.2 collective-permute-done.14
  103.6 63.1 %while.169 = (s32[]{:T(128)}, f32[2,128,128]{2,1,0:T(8,128)S(1)}, f32[2,128,128]{2,1,0:T(8,128)S(1)}, f32[4,2,64,128]{3,2,1,0:T(8,128)S(1)}, f32[4,2,64,1]{2,1,3...) while((s32[]{:T(128)}, f32[2,128,128]{2,1,0:T(8,128)S(1)}, ...), condition=%wide.region_4.6_spmd.clone.clone, body=%wide.region_2.5_spmd.clone.clone.sunk | while | flops 176640128 | bytes 2981140 | solution.py:102
  106.5 9.8 %custom-call.35 = f32[2,1,64,64]{2,3,1,0:T(8,128)S(1)} custom-call(f32[2,1,64,64]{3,2,1,0:T(8,128)S(1)} %fusion.420), custom_call_target="InvertDiagBlocksLowerTriangular" | custom-call | tf_op jit(solution)/shard_map/jvp(vmap())/while/body/eval_jaxpr/jit(_solve_triangular)/triangular_solve/custom-call.1 | solution.py:73
  122.3 9.8 %custom-call.35 = f32[2,1,64,64]{2,3,1,0:T(8,128)S(1)} custom-call(f32[2,1,64,64]{3,2,1,0:T(8,128)S(1)} %fusion.420), custom_call_target="InvertDiagBlocksLowerTriangular" | custom-call | tf_op jit(solution)/shard_map/jvp(vmap())/while/body/eval_jaxpr/jit(_solve_triangular)/triangular_solve/custom-call.1 | solution.py:73
  138.1 9.8 %custom-call.35 = f32[2,1,64,64]{2,3,1,0:T(8,128)S(1)} custom-call(f32[2,1,64,64]{3,2,1,0:T(8,128)S(1)} %fusion.420), custom_call_target="InvertDiagBlocksLowerTriangular" | custom-call | tf_op jit(solution)/shard_map/jvp(vmap())/while/body/eval_jaxpr/jit(_solve_triangular)/triangular_solve/custom-call.1 | solution.py:73
  153.9 9.8 %custom-call.35 = f32[2,1,64,64]{2,3,1,0:T(8,128)S(1)} custom-call(f32[2,1,64,64]{3,2,1,0:T(8,128)S(1)} %fusion.420), custom_call_target="InvertDiagBlocksLowerTriangular" | custom-call | tf_op jit(solution)/shard_map/jvp(vmap())/while/body/eval_jaxpr/jit(_solve_triangular)/triangular_solve/custom-call.1 | solution.py:73
  172.0 5.9 while.166
  179.9 49.5 %all-gather.9.cloned.1.call-done = f32[64,128,128]{2,1,0:T(8,128)} async-done(((f32[2,128,128]{2,1,0:T(8,128)}), f32[64,128,128]{2,1,0:T(8,128)}) %all-gather.9.cloned.1.call-update) | async-done | bytes 4194320 | tf_op jit(solution)/shard_map/all_gather | solution.py:40
  229.4 64.6 %all-gather.11.cloned.1.call-done = f32[64,128,128]{2,1,0:T(8,128)} async-done(((f32[2,128,128]{2,1,0:T(8,128)}), f32[64,128,128]{2,1,0:T(8,128)}) %all-gather.11.cloned.1.call-update) | async-done | bytes 4194320 | tf_op jit(solution)/shard_map/all_gather | solution.py:40
  294.0 80.1 %while.167 = (s32[]{:T(128)}, f32[2,128,128]{2,1,0:T(8,128)S(1)}, f32[2,128,128]{2,1,0:T(8,128)S(1)}, s32[]{:T(128)}, f32[32,2,128,128]{3,2,1,0:T(8,128)}, /*ind...) while((s32[]{:T(128)}, f32[2,128,128]{2,1,0:T(8,128)S(1)}, ...), condition=%wide.region_8.10_spmd.clone, body=%wide.region_7.9_spmd.clone.sunk | while | flops 100827144 | bytes 1706674 | solution.py:53
  374.2 47.8 %all-gather.15.cloned.1.call-done = f32[64,128,128]{2,1,0:T(8,128)} async-done(((f32[2,128,128]{2,1,0:T(8,128)}), f32[64,128,128]{2,1,0:T(8,128)}) %all-gather.15.cloned.1.call-update) | async-done | bytes 4194320 | tf_op jit(solution)/shard_map/all_gather | solution.py:40
  422.0 79.7 %while.168 = (s32[]{:T(128)}, f32[2,128,128]{2,1,0:T(8,128)S(1)}, f32[2,128,128]{2,1,0:T(8,128)S(1)}, s32[]{:T(128)}, f32[32,2,128,128]{3,2,1,0:T(8,128)}, /*ind...) while((s32[]{:T(128)}, f32[2,128,128]{2,1,0:T(8,128)S(1)}, f32[2,128,128]{2,1,0:T(8,128)S(1)}, ...), condition=%wide.region_10.12_spmd.clone, body=%wide.region_9.11_spmd.clone.sunk | while | flops 100827136 | bytes 1706612 | solution.py:53
  514.1 107.1 %while.164 = (s32[]{:T(128)}, f32[2,128,128]{2,1,0:T(8,128)S(1)}, f32[4,2,64,64]{3,2,1,0:T(8,128)}, f32[4,2,128,64]{2,3,1,0:T(8,128)}, f32[4,2,64,64]{3,2,1,0:T(...) while((s32[]{:T(128)}, f32[2,128,128]{2,1,0:T(8,128)S(1)}, ...), condition=%wide.region_13.15_spmd.clone.clone, body=%wide.region_11.14_spmd.clone.clone.sunk | while | flops 126194176 | bytes 3312057 | solution.py:102
  519.2 11.2 %custom-call.33 = f32[2,1,64,64]{2,3,1,0:T(8,128)} custom-call(f32[2,1,64,64]{3,2,1,0:T(8,128)} %select_bitcast_fusion.4), custom_call_target="InvertDiagBlocksLowerTriangular" | custom-call | tf_op jit(solution)/shard_map/jvp(vmap())/while/body/eval_jaxpr/jit(_solve_triangular)/triangular_solve/custom-call.1 | solution.py:73
  530.4 1.8 bitcast_dynamic-update-slice_fusion.22
  546.0 11.2 %custom-call.33 = f32[2,1,64,64]{2,3,1,0:T(8,128)} custom-call(f32[2,1,64,64]{3,2,1,0:T(8,128)} %select_bitcast_fusion.4), custom_call_target="InvertDiagBlocksLowerTriangular" | custom-call | tf_op jit(solution)/shard_map/jvp(vmap())/while/body/eval_jaxpr/jit(_solve_triangular)/triangular_solve/custom-call.1 | solution.py:73
  557.1 1.8 bitcast_dynamic-update-slice_fusion.22
  572.7 11.2 %custom-call.33 = f32[2,1,64,64]{2,3,1,0:T(8,128)} custom-call(f32[2,1,64,64]{3,2,1,0:T(8,128)} %select_bitcast_fusion.4), custom_call_target="InvertDiagBlocksLowerTriangular" | custom-call | tf_op jit(solution)/shard_map/jvp(vmap())/while/body/eval_jaxpr/jit(_solve_triangular)/triangular_solve/custom-call.1 | solution.py:73
  583.9 1.8 bitcast_dynamic-update-slice_fusion.22
  587.1 1.7 bitcast_dynamic-update-slice_fusion.24
  599.5 11.2 %custom-call.33 = f32[2,1,64,64]{2,3,1,0:T(8,128)} custom-call(f32[2,1,64,64]{3,2,1,0:T(8,128)} %select_bitcast_fusion.4), custom_call_target="InvertDiagBlocksLowerTriangular" | custom-call | tf_op jit(solution)/shard_map/jvp(vmap())/while/body/eval_jaxpr/jit(_solve_triangular)/triangular_solve/custom-call.1 | solution.py:73
  610.7 1.8 bitcast_dynamic-update-slice_fusion.22
  625.3 127.3 %while.165 = (s32[]{:T(128)}, f32[2,128,128]{2,1,0:T(8,128)S(1)}, f32[4,2,64,128]{3,2,1,0:T(8,128)}, f32[4,2,64,128]{3,2,1,0:T(8,128)}, f32[4,2,64,128]{3,2,0,1:...) while((s32[]{:T(128)}, f32[2,128,128]{2,1,0:T(8,128)S(1)}, ...), condition=%wide.region_25.27_spmd.clone.clone, body=%wide.region_14.26_spmd.clone.clone.sunk | while | flops 283857920 | bytes 5617773 | solution.py:102
  628.9 9.8 %custom-call.34 = f32[2,1,64,64]{2,3,1,0:T(8,128)S(1)} custom-call(f32[2,1,64,64]{3,2,1,0:T(8,128)S(1)} %select_bitcast_fusion.5), custom_call_target="InvertDiagBlocksLowerTriangular" | custom-call | tf_op jit(solution)/shard_map/transpose(jvp(vmap()))/while/body/eval_jaxpr/jit(_solve_triangular)/triangular_solve | solution.py:73
  650.8 1.8 fusion.380
  660.7 9.8 %custom-call.34 = f32[2,1,64,64]{2,3,1,0:T(8,128)S(1)} custom-call(f32[2,1,64,64]{3,2,1,0:T(8,128)S(1)} %select_bitcast_fusion.5), custom_call_target="InvertDiagBlocksLowerTriangular" | custom-call | tf_op jit(solution)/shard_map/transpose(jvp(vmap()))/while/body/eval_jaxpr/jit(_solve_triangular)/triangular_solve | solution.py:73
  682.6 1.8 fusion.380
  692.5 9.8 %custom-call.34 = f32[2,1,64,64]{2,3,1,0:T(8,128)S(1)} custom-call(f32[2,1,64,64]{3,2,1,0:T(8,128)S(1)} %select_bitcast_fusion.5), custom_call_target="InvertDiagBlocksLowerTriangular" | custom-call | tf_op jit(solution)/shard_map/transpose(jvp(vmap()))/while/body/eval_jaxpr/jit(_solve_triangular)/triangular_solve | solution.py:73
  714.3 1.8 fusion.380
  724.3 9.8 %custom-call.34 = f32[2,1,64,64]{2,3,1,0:T(8,128)S(1)} custom-call(f32[2,1,64,64]{3,2,1,0:T(8,128)S(1)} %select_bitcast_fusion.5), custom_call_target="InvertDiagBlocksLowerTriangular" | custom-call | tf_op jit(solution)/shard_map/transpose(jvp(vmap()))/while/body/eval_jaxpr/jit(_solve_triangular)/triangular_solve | solution.py:73
  746.2 1.8 fusion.380
  763.1 12.7 %all-to-all-start = ((bf16[16,16,512]{2,1,0:T(8,128)(2,1)}), bf16[16,16,512]{2,1,0:T(8,128)(2,1)S(1)}, u32[]{:S(2)}, u32[]{:S(2)}) async-start(bf16[16,16,512]{2,1,0:T(8,128)(2,1)} %bitcast.31), calls=%async_computation | async-start | bytes 524288 | tf_op jit(solution)/shard_map/all_to_all | solution.py:186
  776.6 66.4 %psum.7 = f32[4,512]{1,0:T(4,128)} all-reduce(f32[4,512]{1,0:T(4,128)S(1)} %pad_add_fusion.5), channel_id=1, replica_groups=mesh['ctx'=32,'head'=16] {'ctx'}, use_global_device_ids=true, to_apply=%region_34.36 | all-reduce | flops 2048 | bytes 16384 | tf_op jit(solution)/shard_map/psum | solution.py:189
  (766 shorter events, 363.7 us)
Async XLA Ops:
  7.2 494.6 %copy-start = (f32[2,128,128]{2,1,0:T(8,128)S(1)}, f32[2,128,128]{2,1,0:T(8,128)}, u32[]{:S(2)}) copy-start(f32[2,128,128]{2,1,0:T(8,128)} %param.25) | copy-start | bytes 393220
  7.2 222.2 %all-gather.9.cloned.1.call-start = ((), (), s32[]{:S(2)}) async-start(), calls=%async_computation.1 | async-start | bytes 4325376 | tf_op jit(solution)/shard_map/all_gather | solution.py:40
  8.3 26.1 %collective-permute-start = (bf16[16,512]{1,0:T(8,128)(2,1)S(1)}, bf16[16,512]{1,0:T(8,128)(2,1)S(1)}, u32[]{:S(2)}, u32[]{:S(2)}) collective-permute-start(bf16[16,512]{1,0:T(8,128)(2,1)S(1)} %get-tuple-element.3229), channel_id=1, source_target_pairs={{0,1},{1,0},{2,3},{3,2},{4,5},{5,4},{6,7},{7,6},{8,9},{9,8},{10,11... | collective-permute-start | bytes 49160 | tf_op jit(solution)/shard_map/ppermute | solution.py:27
  15.7 25.2 %collective-permute-start.1 = (bf16[16,512]{1,0:T(8,128)(2,1)S(1)}, bf16[16,512]{1,0:T(8,128)(2,1)S(1)}, u32[]{:S(2)}, u32[]{:S(2)}) collective-permute-start(bf16[16,512]{1,0:T(8,128)(2,1)S(1)} %get-tuple-element.3228), channel_id=1, source_target_pairs={{0,2},{1,3},{2,0},{3,1},{4,6},{5,7},{6,4},{7,5},{8,10},{9,11},{10,... | collective-permute-start | bytes 49160 | tf_op jit(solution)/shard_map/ppermute | solution.py:27
  17.7 27.0 %collective-permute-start.2 = (bf16[16,512]{1,0:T(8,128)(2,1)S(1)}, bf16[16,512]{1,0:T(8,128)(2,1)S(1)}, u32[]{:S(2)}, u32[]{:S(2)}) collective-permute-start(bf16[16,512]{1,0:T(8,128)(2,1)S(1)} %get-tuple-element.3227), channel_id=1, source_target_pairs={{0,3},{1,2},{2,1},{3,0},{4,7},{5,6},{6,5},{7,4},{8,11},{9,10},{10,... | collective-permute-start | bytes 49160 | tf_op jit(solution)/shard_map/ppermute | solution.py:27
  21.1 35.0 %collective-permute-start.3 = (bf16[16,512]{1,0:T(8,128)(2,1)S(1)}, bf16[16,512]{1,0:T(8,128)(2,1)S(1)}, u32[]{:S(2)}, u32[]{:S(2)}) collective-permute-start(bf16[16,512]{1,0:T(8,128)(2,1)S(1)} %get-tuple-element.3226), channel_id=1, source_target_pairs={{0,4},{1,5},{2,6},{3,7},{4,0},{5,1},{6,2},{7,3},{8,12},{9,13},{10,... | collective-permute-start | bytes 49160 | tf_op jit(solution)/shard_map/ppermute | solution.py:27
  27.0 33.7 %collective-permute-start.4 = (bf16[16,512]{1,0:T(8,128)(2,1)S(1)}, bf16[16,512]{1,0:T(8,128)(2,1)S(1)}, u32[]{:S(2)}, u32[]{:S(2)}) collective-permute-start(bf16[16,512]{1,0:T(8,128)(2,1)S(1)} %get-tuple-element.3225), channel_id=1, source_target_pairs={{0,5},{1,4},{2,7},{3,6},{4,1},{5,0},{6,3},{7,2},{8,13},{9,12},{10,... | collective-permute-start | bytes 49160 | tf_op jit(solution)/shard_map/ppermute | solution.py:27
  33.1 70.3 %copy-start.7 = (f32[1,512]{1,0:T(1,128)}, f32[1,512]{1,0:T(1,128)S(1)}, u32[]{:S(2)}) copy-start(f32[1,512]{1,0:T(1,128)S(1)} %get-tuple-element.3232) | copy-start | bytes 6148
  33.2 70.3 %copy-start.9 = (f32[1,512]{1,0:T(1,128)}, f32[1,512]{1,0:T(1,128)S(1)}, u32[]{:S(2)}) copy-start(f32[1,512]{1,0:T(1,128)S(1)} %get-tuple-element.3233) | copy-start | bytes 6148
  33.2 70.3 %copy-start.11 = (f32[1,512]{1,0:T(1,128)}, f32[1,512]{1,0:T(1,128)S(1)}, u32[]{:S(2)}) copy-start(f32[1,512]{1,0:T(1,128)S(1)} %get-tuple-element.3234) | copy-start | bytes 6148
  33.2 70.3 %copy-start.13 = (f32[1,512]{1,0:T(1,128)}, f32[1,512]{1,0:T(1,128)S(1)}, u32[]{:S(2)}) copy-start(f32[1,512]{1,0:T(1,128)S(1)} %get-tuple-element.3235) | copy-start | bytes 6148
  34.5 31.2 %collective-permute-start.5 = (bf16[16,512]{1,0:T(8,128)(2,1)S(1)}, bf16[16,512]{1,0:T(8,128)(2,1)S(1)}, u32[]{:S(2)}, u32[]{:S(2)}) collective-permute-start(bf16[16,512]{1,0:T(8,128)(2,1)S(1)} %get-tuple-element.3224), channel_id=1, source_target_pairs={{0,6},{1,7},{2,4},{3,5},{4,2},{5,3},{6,0},{7,1},{8,14},{9,15},{10,... | collective-permute-start | bytes 49160 | tf_op jit(solution)/shard_map/ppermute | solution.py:27
  40.9 31.2 %collective-permute-start.6 = (bf16[16,512]{1,0:T(8,128)(2,1)S(1)}, bf16[16,512]{1,0:T(8,128)(2,1)S(1)}, u32[]{:S(2)}, u32[]{:S(2)}) collective-permute-start(bf16[16,512]{1,0:T(8,128)(2,1)S(1)} %get-tuple-element.3223), channel_id=1, source_target_pairs={{0,7},{1,6},{2,5},{3,4},{4,3},{5,2},{6,1},{7,0},{8,15},{9,14},{10,... | collective-permute-start | bytes 49160 | tf_op jit(solution)/shard_map/ppermute | solution.py:27
  44.6 32.6 %collective-permute-start.7 = (bf16[16,512]{1,0:T(8,128)(2,1)S(1)}, bf16[16,512]{1,0:T(8,128)(2,1)S(1)}, u32[]{:S(2)}, u32[]{:S(2)}) collective-permute-start(bf16[16,512]{1,0:T(8,128)(2,1)S(1)} %get-tuple-element.3222), channel_id=1, source_target_pairs={{0,8},{1,9},{2,10},{3,11},{4,12},{5,13},{6,14},{7,15},{8,0},{9,1},... | collective-permute-start | bytes 49160 | tf_op jit(solution)/shard_map/ppermute | solution.py:27
  56.0 27.3 %collective-permute-start.8 = (bf16[16,512]{1,0:T(8,128)(2,1)S(1)}, bf16[16,512]{1,0:T(8,128)(2,1)S(1)}, u32[]{:S(2)}, u32[]{:S(2)}) collective-permute-start(bf16[16,512]{1,0:T(8,128)(2,1)S(1)} %get-tuple-element.3221), channel_id=1, source_target_pairs={{0,9},{1,8},{2,11},{3,10},{4,13},{5,12},{6,15},{7,14},{8,1},{9,0},... | collective-permute-start | bytes 49160 | tf_op jit(solution)/shard_map/ppermute | solution.py:27
  60.7 28.3 %collective-permute-start.9 = (bf16[16,512]{1,0:T(8,128)(2,1)S(1)}, bf16[16,512]{1,0:T(8,128)(2,1)S(1)}, u32[]{:S(2)}, u32[]{:S(2)}) collective-permute-start(bf16[16,512]{1,0:T(8,128)(2,1)S(1)} %get-tuple-element.3220), channel_id=1, source_target_pairs={{0,10},{1,11},{2,8},{3,9},{4,14},{5,15},{6,12},{7,13},{8,2},{9,3},... | collective-permute-start | bytes 49160 | tf_op jit(solution)/shard_map/ppermute | solution.py:27
  65.7 26.6 %collective-permute-start.10 = (bf16[16,512]{1,0:T(8,128)(2,1)S(1)}, bf16[16,512]{1,0:T(8,128)(2,1)S(1)}, u32[]{:S(2)}, u32[]{:S(2)}) collective-permute-start(bf16[16,512]{1,0:T(8,128)(2,1)S(1)} %get-tuple-element.3219), channel_id=1, source_target_pairs={{0,11},{1,10},{2,9},{3,8},{4,15},{5,14},{6,13},{7,12},{8,3},{9,2},... | collective-permute-start | bytes 49160 | tf_op jit(solution)/shard_map/ppermute | solution.py:27
  72.2 20.1 %collective-permute-start.11 = (bf16[16,512]{1,0:T(8,128)(2,1)S(1)}, bf16[16,512]{1,0:T(8,128)(2,1)S(1)}, u32[]{:S(2)}, u32[]{:S(2)}) collective-permute-start(bf16[16,512]{1,0:T(8,128)(2,1)S(1)} %get-tuple-element.3218), channel_id=1, source_target_pairs={{0,12},{1,13},{2,14},{3,15},{4,8},{5,9},{6,10},{7,11},{8,4},{9,5},... | collective-permute-start | bytes 49160 | tf_op jit(solution)/shard_map/ppermute | solution.py:27
  77.2 15.1 %collective-permute-start.12 = (bf16[16,512]{1,0:T(8,128)(2,1)S(1)}, bf16[16,512]{1,0:T(8,128)(2,1)S(1)}, u32[]{:S(2)}, u32[]{:S(2)}) collective-permute-start(bf16[16,512]{1,0:T(8,128)(2,1)S(1)} %get-tuple-element.3217), channel_id=1, source_target_pairs={{0,13},{1,12},{2,15},{3,14},{4,9},{5,8},{6,11},{7,10},{8,5},{9,4},... | collective-permute-start | bytes 49160 | tf_op jit(solution)/shard_map/ppermute | solution.py:27
  83.4 9.0 %collective-permute-start.13 = (bf16[16,512]{1,0:T(8,128)(2,1)S(1)}, bf16[16,512]{1,0:T(8,128)(2,1)S(1)}, u32[]{:S(2)}, u32[]{:S(2)}) collective-permute-start(bf16[16,512]{1,0:T(8,128)(2,1)S(1)} %get-tuple-element.3231), channel_id=1, source_target_pairs={{0,14},{1,15},{2,12},{3,13},{4,10},{5,11},{6,8},{7,9},{8,6},{9,7},... | collective-permute-start | bytes 49160 | tf_op jit(solution)/shard_map/ppermute | solution.py:27
  89.0 8.6 %collective-permute-start.14 = (bf16[16,512]{1,0:T(8,128)(2,1)S(1)}, bf16[16,512]{1,0:T(8,128)(2,1)S(1)}, u32[]{:S(2)}, u32[]{:S(2)}) collective-permute-start(bf16[16,512]{1,0:T(8,128)(2,1)S(1)} %get-tuple-element.3216), channel_id=1, source_target_pairs={{0,15},{1,14},{2,13},{3,12},{4,11},{5,10},{6,9},{7,8},{8,7},{9,6},... | collective-permute-start | bytes 49160 | tf_op jit(solution)/shard_map/ppermute | solution.py:27
  97.6 3.4 collective-permute-start.15
  102.3 0.6 copy-start.17
  102.3 1.2 copy-start.18
  102.9 0.7 copy-start.16
  166.7 5.3 copy-start.2
  166.7 5.3 copy-start.3
  167.5 126.5 %all-gather.11.cloned.1.call-start = ((), (), s32[]{:S(2)}) async-start(), calls=%async_computation.2 | async-start | bytes 4325376 | tf_op jit(solution)/shard_map/all_gather | solution.py:40
  177.9 0.7 copy-start.1
  178.5 195.6 %all-gather.13.cloned.1.call-start = ((), (), s32[]{:S(2)}) async-start(), calls=%async_computation.3 | async-start | bytes 4325376 | tf_op jit(solution)/shard_map/all_gather | solution.py:40
  179.3 242.7 %all-gather.15.cloned.1.call-start = ((), (), s32[]{:S(2)}) async-start(), calls=%async_computation.4 | async-start | bytes 4325376 | tf_op jit(solution)/shard_map/all_gather | solution.py:40
  374.1 47.9 %copy-start.4 = (f32[2,128,128]{2,1,0:T(8,128)}, f32[2,128,128]{2,1,0:T(8,128)S(1)}, u32[]{:S(2)}) copy-start(f32[2,128,128]{2,1,0:T(8,128)S(1)} %get-tuple-element.2004) | copy-start | bytes 393220
  625.3 29.9 %copy-start.6 = (f32[4,2,64]{2,1,0:T(2,128)S(1)}, f32[4,2,64]{2,1,0:T(2,128)}, u32[]{:S(2)}) copy-start(f32[4,2,64]{2,1,0:T(2,128)} %get-tuple-element.4315) | copy-start | bytes 6148 | tf_op jit(solution)/shard_map/transpose(jvp(vmap()))/while
  625.3 30.1 %copy-start.5 = (f32[4,2,64]{2,1,0:T(2,128)S(1)}, f32[4,2,64]{2,1,0:T(2,128)}, u32[]{:S(2)}) copy-start(f32[4,2,64]{2,1,0:T(2,128)} %get-tuple-element.4312) | copy-start | bytes 6148 | tf_op jit(solution)/shard_map/transpose(jvp(vmap()))/while
  657.1 29.9 %copy-start.6 = (f32[4,2,64]{2,1,0:T(2,128)S(1)}, f32[4,2,64]{2,1,0:T(2,128)}, u32[]{:S(2)}) copy-start(f32[4,2,64]{2,1,0:T(2,128)} %get-tuple-element.4315) | copy-start | bytes 6148 | tf_op jit(solution)/shard_map/transpose(jvp(vmap()))/while
  657.1 30.1 %copy-start.5 = (f32[4,2,64]{2,1,0:T(2,128)S(1)}, f32[4,2,64]{2,1,0:T(2,128)}, u32[]{:S(2)}) copy-start(f32[4,2,64]{2,1,0:T(2,128)} %get-tuple-element.4312) | copy-start | bytes 6148 | tf_op jit(solution)/shard_map/transpose(jvp(vmap()))/while
  688.9 29.8 %copy-start.6 = (f32[4,2,64]{2,1,0:T(2,128)S(1)}, f32[4,2,64]{2,1,0:T(2,128)}, u32[]{:S(2)}) copy-start(f32[4,2,64]{2,1,0:T(2,128)} %get-tuple-element.4315) | copy-start | bytes 6148 | tf_op jit(solution)/shard_map/transpose(jvp(vmap()))/while
  688.9 30.0 %copy-start.5 = (f32[4,2,64]{2,1,0:T(2,128)S(1)}, f32[4,2,64]{2,1,0:T(2,128)}, u32[]{:S(2)}) copy-start(f32[4,2,64]{2,1,0:T(2,128)} %get-tuple-element.4312) | copy-start | bytes 6148 | tf_op jit(solution)/shard_map/transpose(jvp(vmap()))/while
  720.7 29.8 %copy-start.6 = (f32[4,2,64]{2,1,0:T(2,128)S(1)}, f32[4,2,64]{2,1,0:T(2,128)}, u32[]{:S(2)}) copy-start(f32[4,2,64]{2,1,0:T(2,128)} %get-tuple-element.4315) | copy-start | bytes 6148 | tf_op jit(solution)/shard_map/transpose(jvp(vmap()))/while
  720.7 30.0 %copy-start.5 = (f32[4,2,64]{2,1,0:T(2,128)S(1)}, f32[4,2,64]{2,1,0:T(2,128)}, u32[]{:S(2)}) copy-start(f32[4,2,64]{2,1,0:T(2,128)} %get-tuple-element.4312) | copy-start | bytes 6148 | tf_op jit(solution)/shard_map/transpose(jvp(vmap()))/while
  752.5 6.4 copy-start.8
  752.6 6.4 copy-start.10
  752.6 6.4 copy-start.12
  752.6 6.4 copy-start.14
  759.3 16.6 %copy-start.15 = (f32[4,2,64]{2,1,0:T(2,128)S(1)}, f32[4,2,64]{2,1,0:T(2,128)}, u32[]{:S(2)}) copy-start(f32[4,2,64]{2,1,0:T(2,128)} %get-tuple-element.2034) | copy-start | bytes 6148
  759.3 83.7 %copy-start.19 = (f32[2,256]{1,0:T(2,128)S(1)}, f32[2,256]{1,0:T(2,128)}, u32[]{:S(2)}) copy-start(f32[2,256]{1,0:T(2,128)} %param.23) | copy-start | bytes 6148
  759.3 3.1 collective-permute-start.16
  763.1 80.5 %all-to-all-start = ((bf16[16,16,512]{2,1,0:T(8,128)(2,1)}), bf16[16,16,512]{2,1,0:T(8,128)(2,1)S(1)}, u32[]{:S(2)}, u32[]{:S(2)}) async-start(bf16[16,16,512]{2,1,0:T(8,128)(2,1)} %bitcast.31), calls=%async_computation | async-start | bytes 524288 | tf_op jit(solution)/shard_map/all_to_all | solution.py:186
Sparse Core Ops, SparseCore 0:
  167.6 61.7 all-gather.8
  233.1 60.8 all-gather.10
  297.1 60.9 all-gather.12
  361.1 60.8 all-gather.14
